TPU v7x, 32 devices: a whole 2x2x4 slice. The times are simulated.
32 devices in a mesh: batch: 4 (over y, x), ctx: 8 (over z, core).
Axes of the slice: x: 2, y: 2, z: 4, core: 2. Of those that a mesh axis runs over, the one named last changes fastest.
Arguments:
- hidden: bfloat16 [4, 1024, 768], P('batch', 'ctx'), may hold values from -6 to 6
- cotangent: bfloat16 [4, 1024, 768], P('batch', 'ctx'), may hold values from -6 to 6
- w_qkv: bfloat16 [768, 2304], P(('batch', 'ctx')), may hold values from -3 to 3
- w_proj: bfloat16 [768, 768], P(('batch', 'ctx')), may hold values from -1.25 to 1.25
- w_inner: bfloat16 [768, 2304], P(('batch', 'ctx')), may hold values from -0.21875 to 0.21875
- w_down: bfloat16 [768, 1152], P(('batch', 'ctx')), may hold values from -0.1875 to 0.1875
- norm1_gain: bfloat16 [768], P(('batch', 'ctx')), may hold values from 0.5 to 1.5
- norm2_gain: bfloat16 [768], P(('batch', 'ctx')), may hold values from 0.5 to 1.5
Outputs:
- hidden_out: bfloat16 [4, 1024, 768], P('batch', 'ctx')
- hidden_grad: float32 [4, 1024, 768], P('batch', 'ctx')
- qkv_grad: float32 [768, 2304], P(('batch', 'ctx'))
- proj_grad: float32 [768, 768], P(('batch', 'ctx'))
- inner_grad: float32 [768, 2304], P(('batch', 'ctx'))
- down_grad: float32 [768, 1152], P(('batch', 'ctx'))
- norm1_grad: float32 [768], P(('batch', 'ctx'))
- norm2_grad: float32 [768], P(('batch', 'ctx'))
All inputs are finite; a program needn't handle non-finite values.
Results may differ from a plain program's by a relative error of at most 0.02.
Values may be sent and summed in bfloat16 or wider, within the bound.
A program may use at most 192 MiB of HBM per device.

v0:
```python
import jax
import jax.numpy as jnp
from jax import lax
from jax.sharding import PartitionSpec as P

D = 768
HEADS = 12
HEAD_DIM = 64
FF = 1152
norm_eps = 1e-05
rope_base = 160000.0


def apply_layer_norm(values, gain_vector):
    centre = jnp.mean(values, axis=-1, keepdims=True)
    shifted = values - centre
    spread = jnp.mean(shifted * shifted, axis=-1, keepdims=True)
    inverse = lax.rsqrt(spread + norm_eps)
    normed = shifted * inverse
    return (normed * gain_vector, normed, inverse)


def layer_norm_gradient(upstream, gain_vector, normed, inverse):
    scaled = upstream * gain_vector
    first_mean = jnp.mean(scaled, axis=-1, keepdims=True)
    second_mean = jnp.mean(scaled * normed, axis=-1, keepdims=True)
    return (
        inverse * (scaled - first_mean - normed * second_mean),
        jnp.sum(upstream * normed, axis=0),
    )


def rope_tables(offset, row_count, head_width):
    half_dim = head_width // 2
    position = (offset + jnp.arange(row_count, dtype=jnp.int32)).astype(jnp.float32)
    exponent = jnp.arange(half_dim, dtype=jnp.int32).astype(jnp.float32) * (-2.0 / head_width)
    angles = position[:, None] * jnp.power(rope_base, exponent)[None, :]
    return (jnp.cos(angles), jnp.sin(angles))


def rotate(values, cosine, sine_table, direction):
    half_dim = values.shape[-1] // 2
    front_half = values[..., :half_dim]
    back_half = values[..., half_dim:]
    cos_rows = cosine[:, None, :]
    sin_rows = sine_table[:, None, :] * direction
    return jnp.concatenate(
        [
            front_half * cos_rows - back_half * sin_rows,
            back_half * cos_rows + front_half * sin_rows,
        ],
        axis=-1,
    )


def gelu_parts(act_input):
    normal_cdf = 0.5 * (1.0 + jax.scipy.special.erf(act_input * 0.7071067811865476))
    density = jnp.exp(-0.5 * act_input * act_input) * 0.3989422804014327
    return (act_input * normal_cdf, normal_cdf + act_input * density)


def as_heads(flat_rows):
    return flat_rows.reshape(flat_rows.shape[0], HEADS, HEAD_DIM)


def pair_terms(query_rows, grad_rows, log_rows, delta_rows, key_rows, value_rows, score_scale):
    scores = (
        jnp.einsum("qhd,khd->hqk", query_rows, key_rows, preferred_element_type=jnp.float32)
        * score_scale
    )
    probabilities = jnp.exp(scores - log_rows[..., None])
    grad_dots = jnp.einsum(
        "qhd,khd->hqk", grad_rows, value_rows, preferred_element_type=jnp.float32
    )
    dscore = (probabilities * (grad_dots - delta_rows[..., None])).astype(jnp.bfloat16)
    return (probabilities.astype(jnp.bfloat16), dscore)


def local(hidden, cotangent, w_qkv, w_proj, w_inner, w_down, norm1_gain, norm2_gain):
    token_rows = hidden.shape[1]
    score_scale = HEAD_DIM ** (-0.5)
    full_qkv, full_proj, full_inner, full_down, gain_first, gain_second = (
        lax.all_gather(w_qkv, ("batch", "ctx"), axis=0, tiled=True),
        lax.all_gather(w_proj, ("batch", "ctx"), axis=0, tiled=True),
        lax.all_gather(w_inner, ("batch", "ctx"), axis=0, tiled=True),
        lax.all_gather(w_down, ("batch", "ctx"), axis=0, tiled=True),
        lax.all_gather(norm1_gain, ("batch", "ctx"), axis=0, tiled=True),
        lax.all_gather(norm2_gain, ("batch", "ctx"), axis=0, tiled=True),
    )
    first_norm_gain = gain_first.astype(jnp.float32)
    second_norm_gain = gain_second.astype(jnp.float32)
    input_tokens = hidden[0].astype(jnp.float32)
    first_normed_rows, first_centered_rows, first_inverse_deviation = apply_layer_norm(
        input_tokens, first_norm_gain
    )
    h_one = first_normed_rows.astype(jnp.bfloat16)
    projected = jnp.dot(h_one, full_qkv, preferred_element_type=jnp.float32)
    cosine, sine_table = rope_tables(lax.axis_index("ctx") * token_rows, token_rows, HEAD_DIM)
    query_rot = rotate(as_heads(projected[:, :D]), cosine, sine_table, 1.0).astype(jnp.bfloat16)
    key_flat = (
        rotate(as_heads(projected[:, D : 2 * D]), cosine, sine_table, 1.0)
        .astype(jnp.bfloat16)
        .reshape(token_rows, D)
    )
    value_flat = projected[:, 2 * D :].astype(jnp.bfloat16)
    key_rot = as_heads(key_flat)
    value_rows = as_heads(value_flat)
    zero_heads = jnp.zeros((token_rows, HEADS, HEAD_DIM), jnp.float32)
    piece_rows = (
        lax.all_gather(key_flat, "ctx", axis=0, tiled=True),
        lax.all_gather(value_flat, "ctx", axis=0, tiled=True),
    )
    row_peak = jnp.full((HEADS, token_rows), -jnp.inf, jnp.float32)
    row_total = jnp.zeros((HEADS, token_rows), jnp.float32)
    key_piece = as_heads(piece_rows[0])
    value_piece = as_heads(piece_rows[1])
    scores = (
        jnp.einsum("qhd,khd->hqk", query_rot, key_piece, preferred_element_type=jnp.float32)
        * score_scale
    )
    new_peak = jnp.max(scores, axis=-1)
    row_fade = jnp.exp(row_peak - new_peak)
    probabilities = jnp.exp(scores - new_peak[..., None])
    new_total = row_total * row_fade + jnp.sum(probabilities, axis=-1)
    new_mixture = zero_heads * jnp.transpose(row_fade)[:, :, None] + jnp.einsum(
        "hqk,khd->qhd",
        probabilities.astype(jnp.bfloat16),
        value_piece,
        preferred_element_type=jnp.float32,
    )
    log_total = new_peak + jnp.log(new_total)
    attended = (
        (new_mixture / jnp.transpose(new_total)[:, :, None])
        .reshape(token_rows, D)
        .astype(jnp.bfloat16)
    )
    residual_stream = input_tokens + jnp.dot(
        attended, full_proj, preferred_element_type=jnp.float32
    )
    second_normed_rows, second_centered_rows, second_inverse_deviation = apply_layer_norm(
        residual_stream, second_norm_gain
    )
    h_two = second_normed_rows.astype(jnp.bfloat16)
    inner_all = jnp.dot(h_two, full_inner, preferred_element_type=jnp.float32)
    act_half = inner_all[:, :FF]
    gate_half = inner_all[:, FF:]
    activated, gelu_slope = gelu_parts(act_half)
    middle = (activated * gate_half).astype(jnp.bfloat16)
    output_rows = residual_stream + jnp.einsum(
        "tf,df->td", middle, full_down, preferred_element_type=jnp.float32
    )
    back_qkv, back_proj, back_inner, back_down = (full_qkv, full_proj, full_inner, full_down)
    upstream = cotangent[0]
    d_middle = jnp.dot(upstream, back_down, preferred_element_type=jnp.float32)
    d_inner = jnp.concatenate(
        [d_middle * gate_half * gelu_slope, d_middle * activated], axis=-1
    ).astype(jnp.bfloat16)
    second_hidden_gradient = jnp.einsum(
        "te,de->td", d_inner, back_inner, preferred_element_type=jnp.float32
    )
    residual_norm_gradient, second_gain_portion = layer_norm_gradient(
        second_hidden_gradient, second_norm_gain, second_centered_rows, second_inverse_deviation
    )
    d_resid = upstream.astype(jnp.float32) + residual_norm_gradient
    d_resid_low = d_resid.astype(jnp.bfloat16)
    d_attended = jnp.einsum(
        "td,ed->te", d_resid_low, back_proj, preferred_element_type=jnp.float32
    ).astype(jnp.bfloat16)
    grad_heads = as_heads(d_attended)
    row_delta = jnp.transpose(
        jnp.sum(grad_heads.astype(jnp.float32) * as_heads(attended).astype(jnp.float32), axis=-1)
    )
    log_whole, delta_whole = (
        lax.all_gather(log_total, "ctx", axis=1, tiled=True),
        lax.all_gather(row_delta, "ctx", axis=1, tiled=True),
    )
    piece_rows = (
        lax.all_gather(key_flat, "ctx", axis=0, tiled=True),
        lax.all_gather(value_flat, "ctx", axis=0, tiled=True),
    )
    key_part = as_heads(piece_rows[0])
    value_part = as_heads(piece_rows[1])
    probs_low, dscore = pair_terms(
        query_rot, grad_heads, log_total, row_delta, key_part, value_part, score_scale
    )
    query_grad = (
        jnp.einsum("hqk,khd->qhd", dscore, key_part, preferred_element_type=jnp.float32)
        * score_scale
    )
    piece_rows = (
        lax.all_gather(query_rot.reshape(token_rows, D), "ctx", axis=0, tiled=True),
        lax.all_gather(d_attended, "ctx", axis=0, tiled=True),
    )
    query_part = as_heads(piece_rows[0])
    grad_part = as_heads(piece_rows[1])
    probs_low, dscore = pair_terms(
        query_part, grad_part, log_whole, delta_whole, key_rot, value_rows, score_scale
    )
    key_sum = (
        jnp.einsum("hqk,qhd->khd", dscore, query_part, preferred_element_type=jnp.float32)
        * score_scale
    )
    value_sum = jnp.einsum("hqk,qhd->khd", probs_low, grad_part, preferred_element_type=jnp.float32)
    d_query = rotate(query_grad, cosine, sine_table, -1.0)
    d_key = rotate(key_sum, cosine, sine_table, -1.0)
    d_projected = jnp.concatenate(
        [
            d_query.reshape(token_rows, D),
            d_key.reshape(token_rows, D),
            value_sum.reshape(token_rows, D),
        ],
        axis=-1,
    ).astype(jnp.bfloat16)
    first_hidden_gradient = jnp.einsum(
        "te,de->td", d_projected, back_qkv, preferred_element_type=jnp.float32
    )
    input_norm_gradient, first_gain_portion = layer_norm_gradient(
        first_hidden_gradient, first_norm_gain, first_centered_rows, first_inverse_deviation
    )
    input_grad = d_resid + input_norm_gradient

    def grad_rows(start, count):
        return jnp.concatenate(
            [
                jnp.einsum("td,te->de", h_one, d_projected, preferred_element_type=jnp.float32),
                jnp.einsum("te,td->ed", attended, d_resid_low, preferred_element_type=jnp.float32),
                jnp.einsum("td,te->de", h_two, d_inner, preferred_element_type=jnp.float32),
                jnp.einsum("td,tf->df", upstream, middle, preferred_element_type=jnp.float32),
                first_gain_portion[:, None],
                second_gain_portion[:, None],
            ],
            axis=1,
        )

    owned_rows = D // lax.axis_size(("batch", "ctx"))
    grad_share = lax.psum_scatter(
        grad_rows(jnp.int32(0), owned_rows * lax.axis_size(("batch", "ctx"))),
        ("batch", "ctx"),
        scatter_dimension=0,
        tiled=True,
    )
    qkv_share = grad_share[:, : 3 * D]
    proj_share = grad_share[:, 3 * D : 4 * D]
    inner_share = grad_share[:, 4 * D : 4 * D + 2 * FF]
    down_share = grad_share[:, 4 * D + 2 * FF : 4 * D + 3 * FF]
    first_share = grad_share[:, 4 * D + 3 * FF]
    second_share = grad_share[:, 4 * D + 3 * FF + 1]
    return (
        output_rows.astype(jnp.bfloat16)[None],
        input_grad[None],
        qkv_share,
        proj_share,
        inner_share,
        down_share,
        first_share,
        second_share,
    )


def solution(mesh):
    placed = (
        P("batch", "ctx", None),
        P("batch", "ctx", None),
        P(("batch", "ctx"), None),
        P(("batch", "ctx"), None),
        P(("batch", "ctx"), None),
        P(("batch", "ctx"), None),
        P(("batch", "ctx")),
        P(("batch", "ctx")),
    )
    return jax.shard_map(
        local,
        mesh=mesh,
        in_specs=placed,
        out_specs=(
            P("batch", "ctx", None),
            P("batch", "ctx", None),
            P(("batch", "ctx"), None),
            P(("batch", "ctx"), None),
            P(("batch", "ctx"), None),
            P(("batch", "ctx"), None),
            P(("batch", "ctx")),
            P(("batch", "ctx")),
        ),
        check_vma=False,
    )
```

profile of v0, /device:TPU:0, one launch (start us, length us, event | category | flops | bytes accessed | tf_op | source)
XLA Modules:
  0.0 641.2 jit_solution(14519602445404281982)
XLA Ops:
  9.6 42.2 %all-reduce.2 = (bf16[768]{0:T(1024)(128)(2,1)S(1)}, bf16[768]{0:T(1024)(128)(2,1)S(1)}) all-reduce(bf16[768]{0:T(1024)(128)(2,1)S(1)} %dynamic-update-slice, bf16[768]{0:T(1024)(128)(2,1)S(1)} %dynamic-update-slice.1), channel_id=1, replica_groups=mesh['batch'=4,'ctx'=8] {'batch','ctx'}, use_global_device_ids=true, to_apply=%add | all-reduce | flops 1536 | bytes 6144
  54.8 19.1 %all-gather.9.cloned.1.call-done = bf16[768,2304]{1,0:T(8,128)(2,1)} async-done(((bf16[24,2304]{1,0:T(8,128)(2,1)}), bf16[768,2304]{1,0:T(8,128)(2,1)}) %all-gather.9.cloned.1.call-update) | async-done | bytes 3538960 | tf_op jit(solution)/shard_map/all_gather | solution.py:83
  73.9 2.8 fusion.79
  82.0 22.7 %all-gather.11.cloned.1.call-done = bf16[1024,768]{0,1:T(8,128)(2,1)} async-done(((bf16[128,768]{0,1:T(8,128)(2,1)}), bf16[1024,768]{0,1:T(8,128)(2,1)}) %all-gather.11.cloned.1.call-update) | async-done | bytes 1572880 | tf_op jit(solution)/shard_map/all_gather | solution.py:110
  109.9 21.1 %all-gather.13.cloned.1.call-done = bf16[1024,768]{1,0:T(8,128)(2,1)} async-done(((bf16[128,768]{1,0:T(8,128)(2,1)}), bf16[1024,768]{1,0:T(8,128)(2,1)}) %all-gather.13.cloned.1.call-update) | async-done | bytes 1572880 | tf_op jit(solution)/shard_map/all_gather | solution.py:111
  132.7 4.8 fusion.35
  137.5 49.6 %all-gather.15.cloned.1.call-done = bf16[768,768]{1,0:T(8,128)(2,1)} async-done(((bf16[24,768]{1,0:T(8,128)(2,1)}), bf16[768,768]{1,0:T(8,128)(2,1)}) %all-gather.15.cloned.1.call-update) | async-done | bytes 1179664 | tf_op jit(solution)/shard_map/all_gather | solution.py:84
  189.1 59.9 %all-gather.17.cloned.1.call-done = bf16[768,2304]{1,0:T(8,128)(2,1)} async-done(((bf16[24,2304]{1,0:T(8,128)(2,1)}), bf16[768,2304]{1,0:T(8,128)(2,1)}) %all-gather.17.cloned.1.call-update) | async-done | bytes 3538960 | tf_op jit(solution)/shard_map/all_gather | solution.py:85
  249.0 2.7 fusion.81
  251.6 54.4 %all-gather.19.cloned.1.call-done = bf16[768,1152]{1,0:T(8,128)(2,1)} async-done(((bf16[24,1152]{1,0:T(8,128)(2,1)}), bf16[768,1152]{1,0:T(8,128)(2,1)}) %all-gather.19.cloned.1.call-update) | async-done | bytes 1769488 | tf_op jit(solution)/shard_map/all_gather | solution.py:86
  314.4 15.1 %all_gather.47 = f32[12,1024]{1,0:T(8,128)} all-gather(f32[12,128]{1,0:T(8,128)S(1)} %get-tuple-element.36), channel_id=1, replica_groups=mesh['batch'=4,'ctx'=8] {'ctx'}, dimensions={1}, use_global_device_ids=true | all-gather | bytes 55296 | tf_op jit(solution)/shard_map/all_gather | solution.py:174
  329.6 15.2 %all_gather.49 = f32[12,1024]{1,0:T(8,128)} all-gather(f32[12,128]{1,0:T(8,128)S(1)} %bitcast.128), channel_id=1, replica_groups=mesh['batch'=4,'ctx'=8] {'ctx'}, dimensions={1}, use_global_device_ids=true | all-gather | bytes 55296 | tf_op jit(solution)/shard_map/all_gather | solution.py:175
  345.3 3.8 convolution_bitcast_fusion
  349.1 4.1 fusion.59
  353.2 5.1 fusion.85
  358.4 7.3 %fusion.23 = f32[128,12,64]{0,2,1:T(8,128)} fusion(bf16[1024,12,64]{0,2,1:T(8,128)(2,1)} %bitcast.114, f32[12,128,1024]{2,1,0:T(8,128)} %copy-done, f32[12,128]{1,0:T(8,128)S(1)} %bitcast.129, f32[12,128]{1,0:T(8,128)} %copy-done.21, bf16[128,12,64]{0,2,1:T(8,128)(2,1)} %bitcast.120, bf16[1024,12,64]{0,2,1:T(8,128)(2,1)} %bitcast.110), kind=kOutput, calls=%fused_computation.25 | convolution fusion | flops 410615808 | bytes 10039296 | tf_op jit(solution)/shard_map/hqk,khd->qhd/dot_general | solution.py:187
  365.6 2.6 copy.29
  368.2 4.5 fusion.28
  372.7 8.9 %fusion.21 = f32[128,12,64]{0,2,1:T(8,128)} fusion(bf16[1024,12,64]{0,2,1:T(8,128)(2,1)} %bitcast.116, f32[12,1024,128]{2,1,0:T(8,128)} %fusion.85, f32[12,1024]{1,0:T(8,128)} %all_gather.49, f32[12,1024]{1,0:T(8,128)} %all_gather.47, bf16[1024,12,64]{0,2,1:T(8,128)(2,1)} %bitcast.106, bf16[128,12,64]{0,2,1:T(8,128)(2,1)} %bitcast.127), kind=kOutput, calls=%fused_computation.23 | convolution fusion | flops 410615808 | bytes 10125312 | tf_op jit(solution)/shard_map/hqk,qhd->khd/dot_general | solution.py:200
  383.0 4.1 fusion.61
  387.1 2.6 fusion.57
  390.6 22.2 %concatenate.31 = f32[768,6530]{1,0:T(8,128)} concatenate(f32[768,2304]{1,0:T(8,128)} %fusion.61, f32[768,768]{1,0:T(8,128)S(1)} %fusion.66, f32[768,2304]{1,0:T(8,128)} %fusion.59, f32[768,1152]{1,0:T(8,128)} %convolution_bitcast_fusion, f32[768,1]{1,0:T(8,128)} %broadcast_in_dim.18, f32[768,1]{1,0:T(8,128)} %broadcast_in_dim.19), dimensions={1} | concatenate | bytes 40120320 | tf_op jit(solution)/shard_map/concatenate | solution.py:223
  414.1 2.9 fusion.31
  417.9 210.3 %reduce-scatter.2.cloned.1.call-done = f32[24,6530]{1,0:T(8,128)} async-done(((f32[768,6530]{1,0:T(8,128)}), f32[24,6530]{1,0:T(8,128)}) %reduce-scatter.2.cloned.1.call-update) | async-done | bytes 626896 | tf_op jit(solution)/shard_map/reduce_scatter | solution.py:236
  (132 shorter events, 39.0 us)
Async XLA Ops:
  7.2 66.8 %all-gather.9.cloned.1.call-start = ((), (), s32[]{:S(2)}) async-start(), calls=%async_computation.1 | async-start | bytes 3649536 | tf_op jit(solution)/shard_map/all_gather | solution.py:83
  7.9 96.8 %all-gather.11.cloned.1.call-start = ((), (), s32[]{:S(2)}) async-start(), calls=%async_computation.2 | async-start | bytes 1769472 | tf_op jit(solution)/shard_map/all_gather | solution.py:110
  52.9 23.9 %copy-start.22 = (f32[128]{0:T(128)}, f32[128]{0:T(128)S(1)}, u32[]{:S(2)}) copy-start(f32[128]{0:T(128)S(1)} %broadcast_multiply_fusion.6) | copy-start | bytes 1540
  54.1 22.7 %copy-start.26 = (f32[128]{0:T(128)}, f32[128]{0:T(128)S(1)}, u32[]{:S(2)}) copy-start(f32[128]{0:T(128)S(1)} %add_rsqrt_fusion.1) | copy-start | bytes 1540
  54.8 22.3 %copy-start.20 = (f32[128,32]{0,1:T(8,128)}, f32[128,32]{0,1:T(8,128)S(1)}, u32[]{:S(2)}) copy-start(f32[128,32]{0,1:T(8,128)S(1)} %get-tuple-element.40) | copy-start | bytes 49156
  78.6 52.3 %all-gather.13.cloned.1.call-start = ((), (), s32[]{:S(2)}) async-start(), calls=%async_computation.3 | async-start | bytes 1769472 | tf_op jit(solution)/shard_map/all_gather | solution.py:111
  79.4 107.7 %all-gather.15.cloned.1.call-start = ((), (), s32[]{:S(2)}) async-start(), calls=%async_computation.4 | async-start | bytes 1216512 | tf_op jit(solution)/shard_map/all_gather | solution.py:84
  80.0 169.0 %all-gather.17.cloned.1.call-start = ((), (), s32[]{:S(2)}) async-start(), calls=%async_computation.5 | async-start | bytes 3649536 | tf_op jit(solution)/shard_map/all_gather | solution.py:85
  80.6 225.5 %all-gather.19.cloned.1.call-start = ((), (), s32[]{:S(2)}) async-start(), calls=%async_computation.6 | async-start | bytes 1824768 | tf_op jit(solution)/shard_map/all_gather | solution.py:86
  81.2 272.1 %all-gather.21.cloned.1.call-start = ((), (), s32[]{:S(2)}) async-start(), calls=%async_computation.7 | async-start | bytes 1769472 | tf_op jit(solution)/shard_map/all_gather | solution.py:191
  81.9 283.7 %all-gather.23.cloned.1.call-start = ((), (), s32[]{:S(2)}) async-start(), calls=%async_computation.8 | async-start | bytes 1769472 | tf_op jit(solution)/shard_map/all_gather | solution.py:192
  109.9 204.6 %copy-start.21 = (f32[12,128]{1,0:T(8,128)}, f32[12,128]{1,0:T(8,128)S(1)}, u32[]{:S(2)}) copy-start(f32[12,128]{1,0:T(8,128)S(1)} %get-tuple-element.36) | copy-start | bytes 18436
  132.7 4.8 copy-start.8
  132.7 54.4 %copy-start.1 = (bf16[1,128,768]{2,1,0:T(8,128)(2,1)S(1)}, bf16[1,128,768]{2,1,0:T(8,128)(2,1)}, u32[]{:S(2)}) copy-start(bf16[1,128,768]{2,1,0:T(8,128)(2,1)} %param.8) | copy-start | bytes 589828
  188.9 117.2 %copy-start.13 = (bf16[1,128,768]{2,1,0:T(8,128)(2,1)S(1)}, bf16[1,128,768]{2,1,0:T(8,128)(2,1)}, u32[]{:S(2)}) copy-start(bf16[1,128,768]{2,1,0:T(8,128)(2,1)} %param.9) | copy-start | bytes 589828
  188.9 121.2 %copy-start.24 = (f32[128]{0:T(128)}, f32[128]{0:T(128)S(1)}, u32[]{:S(2)}) copy-start(f32[128]{0:T(128)S(1)} %broadcast_multiply_fusion.5) | copy-start | bytes 1540
  189.1 121.0 %copy-start.28 = (f32[128]{0:T(128)}, f32[128]{0:T(128)S(1)}, u32[]{:S(2)}) copy-start(f32[128]{0:T(128)S(1)} %add_rsqrt_fusion) | copy-start | bytes 1540
  251.6 56.7 %copy-start.3 = (f32[128,2304]{1,0:T(8,128)}, f32[128,2304]{1,0:T(8,128)S(1)}, u32[]{:S(2)}) copy-start(f32[128,2304]{1,0:T(8,128)S(1)} %fusion.81) | copy-start | bytes 3538948
  311.5 316.7 %reduce-scatter.2.cloned.1.call-start = ((), (), s32[]{:S(2)}) async-start(), calls=%async_computation.9 | async-start | bytes 21086208 | tf_op jit(solution)/shard_map/reduce_scatter | solution.py:236
  313.5 16.1 %copy-start.14 = (bf16[128,768]{0,1:T(8,128)(2,1)}, bf16[128,768]{0,1:T(8,128)(2,1)S(1)}, u32[]{:S(2)}) copy-start(bf16[128,768]{0,1:T(8,128)(2,1)S(1)} %copy.28) | copy-start | bytes 589828
  344.8 4.2 copy-start.25
  344.8 4.2 copy-start.29
  372.7 10.3 %copy-start.23 = (f32[128]{0:T(128)S(1)}, f32[128]{0:T(128)}, u32[]{:S(2)}) copy-start(f32[128]{0:T(128)} %copy-done.22) | copy-start | bytes 1540
  372.7 10.3 %copy-start.27 = (f32[128]{0:T(128)S(1)}, f32[128]{0:T(128)}, u32[]{:S(2)}) copy-start(f32[128]{0:T(128)} %copy-done.26) | copy-start | bytes 1540
  (16 other events, 44.7 us)
Sparse Core Ops, SparseCore 0:
  11.0 62.9 all-gather.8
  78.8 25.8 all-gather.10
  106.9 24.0 all-gather.12
  133.9 53.2 all-gather.14
  190.0 58.9 all-gather.16
  251.7 54.3 all-gather.18
  308.2 26.2 all-gather.20
  336.8 24.9 all-gather.22
  413.0 215.2 reduce-scatter.1
where the time goes:
time: 642 us; the launch traced here: 641 us
  waiting for transfers between devices  439 us (68%)
  blocking collectives  72.5 us (11%)
  matrix products  62.9 us (10%)
  local copies, waits for them, and re-layouts  43 us (7%)
  between operations  14.3 us (2%)
  other arithmetic  8.55 us (1%)
    reduce_scatter x1, waiting for transfers between devices, local(): lax.psum_scatter(grad_rows(jnp.int32(0), owned_rows * lax.axis_size(('bat...  210 us
    all_gather x1, waiting for transfers between devices, local(): lax.all_gather(w_inner, ('batch', 'ctx'), axis=0, tiled=True)  59.9 us
    all_gather x1, waiting for transfers between devices, local(): lax.all_gather(w_down, ('batch', 'ctx'), axis=0, tiled=True)  54.4 us
    all_gather x1, waiting for transfers between devices, local(): lax.all_gather(w_proj, ('batch', 'ctx'), axis=0, tiled=True)  49.6 us
    unnamed x1, blocking collectives  42.2 us
    all_gather x1, waiting for transfers between devices, local(): lax.all_gather(key_flat, 'ctx', axis=0, tiled=True)  22.7 us
    concatenate x1, local copies, waits for them, and re-layouts, grad_rows(): jnp.concatenate([jnp.einsum('td,te->de', h_one, d_projected, preferred_el...  22.2 us
    all_gather x1, waiting for transfers between devices, local(): lax.all_gather(value_flat, 'ctx', axis=0, tiled=True)  21.1 us
  transfers between devices with their start and end apart: 9, of which 7 were waited for; matrix products, arithmetic and copies ran while one was open for 8% of the time, Pallas kernels for 0%

commit v1 on v0

--- a/solution.py
+++ b/solution.py
@@ -9,6 +9,18 @@
 FF = 1152
 norm_eps = 1e-05
 rope_base = 160000.0
+
+
+def collect(array, axis, dim):
+    ways, here = (lax.axis_size(axis), lax.axis_index(axis))
+    grown, reach = (array, 1)
+    while reach < ways:
+        theirs = lax.ppermute(grown, axis, [(d, d ^ reach) for d in range(ways)])
+        mine_first = jnp.concatenate([grown, theirs], axis=dim)
+        theirs_first = jnp.concatenate([theirs, grown], axis=dim)
+        grown = jnp.where(here & reach == 0, mine_first, theirs_first)
+        reach = 2 * reach
+    return grown
 
 
 def apply_layer_norm(values, gain_vector):
@@ -81,7 +93,7 @@
     score_scale = HEAD_DIM ** (-0.5)
     full_qkv, full_proj, full_inner, full_down, gain_first, gain_second = (
         lax.all_gather(w_qkv, ("batch", "ctx"), axis=0, tiled=True),
-        lax.all_gather(w_proj, ("batch", "ctx"), axis=0, tiled=True),
+        collect(w_proj, ("batch", "ctx"), 0),
         lax.all_gather(w_inner, ("batch", "ctx"), axis=0, tiled=True),
         lax.all_gather(w_down, ("batch", "ctx"), axis=0, tiled=True),
         lax.all_gather(norm1_gain, ("batch", "ctx"), axis=0, tiled=True),

time: 642 us -> 595 us (0.927)
  waiting for transfers between devices: 439 us -> 387 us
    all_gather x1 -> x0, waiting for transfers between devices: 49.6 us -> none  [local(): lax.all_gather(w_proj, ('batch', 'ctx'), axis=0, tiled=True)]
    ppermute x0 -> x5, waiting for transfers between devices: none -> 27.5 us  [collect(): theirs = lax.ppermute(grown, axis, [(d, d ^ reach) for d in range(ways)])]
    all_gather x1, waiting for transfers between devices: 22.7 us -> 0.02 us  [local(): lax.all_gather(key_flat, 'ctx', axis=0, tiled=True)]
  transfers between devices with their start and end apart: 9 -> 13, of which waited for: 7 -> 9; matrix products, arithmetic and copies ran while one was open for 8% -> 9% of each run, Pallas kernels for 0% -> 0%
where the time goes in v1:
time: 595 us; the launch traced here: 594 us
  waiting for transfers between devices  387 us (65%)
  blocking collectives  72.6 us (12%)
  matrix products  61.8 us (10%)
  local copies, waits for them, and re-layouts  43.2 us (7%)
  between operations  14.7 us (2%)
  other arithmetic  8.84 us (1%)
    reduce_scatter x1, waiting for transfers between devices, local(): lax.psum_scatter(grad_rows(jnp.int32(0), owned_rows * lax.axis_size(('bat...  211 us
    all_gather x1, waiting for transfers between devices, local(): lax.all_gather(w_inner, ('batch', 'ctx'), axis=0, tiled=True)  54.7 us
    all_gather x1, waiting for transfers between devices, local(): lax.all_gather(w_down, ('batch', 'ctx'), axis=0, tiled=True)  54.4 us
    unnamed x1, blocking collectives  42.2 us
    ppermute x5, waiting for transfers between devices, collect(): theirs = lax.ppermute(grown, axis, [(d, d ^ reach) for d in range(ways)])  27.5 us
    concatenate x1, local copies, waits for them, and re-layouts, grad_rows(): jnp.concatenate([jnp.einsum('td,te->de', h_one, d_projected, preferred_el...  21.7 us
    all_gather x1, waiting for transfers between devices, local(): lax.all_gather(w_qkv, ('batch', 'ctx'), axis=0, tiled=True)  19.1 us
    all_gather x1, waiting for transfers between devices, local(): lax.all_gather(value_flat, 'ctx', axis=0, tiled=True)  18.6 us
  transfers between devices with their start and end apart: 13, of which 9 were waited for; matrix products, arithmetic and copies ran while one was open for 9% of the time, Pallas kernels for 0%

profile of v1, /device:TPU:0, one launch (start us, length us, event | category | flops | bytes accessed | tf_op | source)
XLA Modules:
  0.0 593.8 jit_solution(10553032929334739325)
XLA Ops:
  9.7 42.2 %all-reduce.2 = (bf16[768]{0:T(1024)(128)(2,1)S(1)}, bf16[768]{0:T(1024)(128)(2,1)S(1)}) all-reduce(bf16[768]{0:T(1024)(128)(2,1)S(1)} %dynamic-update-slice, bf16[768]{0:T(1024)(128)(2,1)S(1)} %dynamic-update-slice.1), channel_id=1, replica_groups=mesh['batch'=4,'ctx'=8] {'batch','ctx'}, use_global_device_ids=true, to_apply=%add | all-reduce | flops 1536 | bytes 6144
  54.8 19.1 %all-gather.8.cloned.1.call-done = bf16[768,2304]{1,0:T(8,128)(2,1)} async-done(((bf16[24,2304]{1,0:T(8,128)(2,1)}), bf16[768,2304]{1,0:T(8,128)(2,1)}) %all-gather.8.cloned.1.call-update) | async-done | bytes 3538960 | tf_op jit(solution)/shard_map/all_gather | solution.py:95
  73.9 2.8 fusion.81
  82.8 3.6 collective-permute-done.1
  87.5 15.8 %collective-permute-done.2 = bf16[96,768]{1,0:T(8,128)(2,1)S(1)} collective-permute-done((bf16[96,768]{1,0:T(8,128)(2,1)S(1)}, bf16[96,768]{1,0:T(8,128)(2,1)S(1)}, u32[]{:S(2)}, u32[]{:S(2)}) %collective-permute-start.2) | collective-permute-done | bytes 147488 | tf_op jit(solution)/shard_map/ppermute | solution.py:18
  104.8 7.2 %collective-permute-done.3 = bf16[192,768]{1,0:T(8,128)(2,1)S(1)} collective-permute-done((bf16[192,768]{1,0:T(8,128)(2,1)S(1)}, bf16[192,768]{1,0:T(8,128)(2,1)S(1)}, u32[]{:S(2)}, u32[]{:S(2)}) %collective-permute-start.3) | collective-permute-done | bytes 294944 | tf_op jit(solution)/shard_map/ppermute | solution.py:18
  114.5 2.5 multiply_reduce_fusion
  119.7 18.6 %all-gather.12.cloned.1.call-done = bf16[1024,768]{1,0:T(8,128)(2,1)} async-done(((bf16[128,768]{1,0:T(8,128)(2,1)}), bf16[1024,768]{1,0:T(8,128)(2,1)}) %all-gather.12.cloned.1.call-update) | async-done | bytes 1572880 | tf_op jit(solution)/shard_map/all_gather | solution.py:123
  140.1 4.8 fusion.35
  145.8 54.7 %all-gather.14.cloned.1.call-done = bf16[768,2304]{1,0:T(8,128)(2,1)} async-done(((bf16[24,2304]{1,0:T(8,128)(2,1)}), bf16[768,2304]{1,0:T(8,128)(2,1)}) %all-gather.14.cloned.1.call-update) | async-done | bytes 3538960 | tf_op jit(solution)/shard_map/all_gather | solution.py:97
  200.4 2.7 fusion.83
  203.1 54.4 %all-gather.16.cloned.1.call-done = bf16[768,1152]{1,0:T(8,128)(2,1)} async-done(((bf16[24,1152]{1,0:T(8,128)(2,1)}), bf16[768,1152]{1,0:T(8,128)(2,1)}) %all-gather.16.cloned.1.call-update) | async-done | bytes 1769488 | tf_op jit(solution)/shard_map/all_gather | solution.py:98
  265.9 15.2 %all_gather.43 = f32[12,1024]{1,0:T(8,128)} all-gather(f32[12,128]{1,0:T(8,128)S(1)} %get-tuple-element.36), channel_id=1, replica_groups=mesh['batch'=4,'ctx'=8] {'ctx'}, dimensions={1}, use_global_device_ids=true | all-gather | bytes 55296 | tf_op jit(solution)/shard_map/all_gather | solution.py:186
  281.2 15.2 %all_gather.45 = f32[12,1024]{1,0:T(8,128)} all-gather(f32[12,128]{1,0:T(8,128)S(1)} %bitcast.126), channel_id=1, replica_groups=mesh['batch'=4,'ctx'=8] {'ctx'}, dimensions={1}, use_global_device_ids=true | all-gather | bytes 55296 | tf_op jit(solution)/shard_map/all_gather | solution.py:187
  300.4 4.1 fusion.59
  304.5 5.1 fusion.87
  309.6 7.3 %fusion.23 = f32[128,12,64]{0,2,1:T(8,128)} fusion(bf16[1024,12,64]{0,2,1:T(8,128)(2,1)} %bitcast.110, f32[12,128,1024]{2,1,0:T(8,128)} %copy-done, f32[12,128]{1,0:T(8,128)S(1)} %bitcast.127, f32[12,128]{1,0:T(8,128)} %copy-done.28, bf16[128,12,64]{0,2,1:T(8,128)(2,1)} %bitcast.118, bf16[1024,12,64]{0,2,1:T(8,128)(2,1)} %bitcast.106), kind=kOutput, calls=%fused_computation.25 | convolution fusion | flops 410615808 | bytes 10039296 | tf_op jit(solution)/shard_map/hqk,khd->qhd/dot_general | solution.py:199
  316.9 2.6 copy.29
  319.5 5.1 fusion.28
  324.6 8.8 %fusion.21 = f32[128,12,64]{0,2,1:T(8,128)} fusion(bf16[1024,12,64]{0,2,1:T(8,128)(2,1)} %bitcast.112, f32[12,1024,128]{2,1,0:T(8,128)} %fusion.87, f32[12,1024]{1,0:T(8,128)} %all_gather.45, f32[12,1024]{1,0:T(8,128)} %all_gather.43, bf16[1024,12,64]{0,2,1:T(8,128)(2,1)} %bitcast.104, bf16[128,12,64]{0,2,1:T(8,128)(2,1)} %bitcast.125), kind=kOutput, calls=%fused_computation.23 | convolution fusion | flops 410615808 | bytes 10125312 | tf_op jit(solution)/shard_map/hqk,qhd->khd/dot_general | solution.py:212
  335.0 5.3 fusion.61
  340.2 2.6 fusion.57
  343.7 21.7 %concatenate.71 = f32[768,6530]{1,0:T(8,128)} concatenate(f32[768,2304]{1,0:T(8,128)} %fusion.61, f32[768,768]{1,0:T(8,128)} %fusion.66, f32[768,2304]{1,0:T(8,128)} %fusion.59, f32[768,1152]{1,0:T(8,128)S(1)} %convolution_bitcast_fusion, f32[768,1]{1,0:T(8,128)} %broadcast_in_dim.18, f32[768,1]{1,0:T(8,128)} %broadcast_in_dim.19), dimensions={1} | concatenate | bytes 40120320 | tf_op jit(solution)/shard_map/concatenate | solution.py:235
  369.7 210.9 %reduce-scatter.2.cloned.1.call-done = f32[24,6530]{1,0:T(8,128)} async-done(((f32[768,6530]{1,0:T(8,128)}), f32[24,6530]{1,0:T(8,128)}) %reduce-scatter.2.cloned.1.call-update) | async-done | bytes 626896 | tf_op jit(solution)/shard_map/reduce_scatter | solution.py:248
  (157 shorter events, 46.8 us)
Async XLA Ops:
  7.2 66.8 %all-gather.8.cloned.1.call-start = ((), (), s32[]{:S(2)}) async-start(), calls=%async_computation.1 | async-start | bytes 3649536 | tf_op jit(solution)/shard_map/all_gather | solution.py:95
  7.9 106.6 %all-gather.10.cloned.1.call-start = ((), (), s32[]{:S(2)}) async-start(), calls=%async_computation.2 | async-start | bytes 1769472 | tf_op jit(solution)/shard_map/all_gather | solution.py:122
  52.9 23.8 %copy-start.29 = (f32[128]{0:T(128)}, f32[128]{0:T(128)S(1)}, u32[]{:S(2)}) copy-start(f32[128]{0:T(128)S(1)} %broadcast_multiply_fusion.6) | copy-start | bytes 1540
  54.1 22.7 %copy-start.33 = (f32[128]{0:T(128)}, f32[128]{0:T(128)S(1)}, u32[]{:S(2)}) copy-start(f32[128]{0:T(128)S(1)} %add_rsqrt_fusion.1) | copy-start | bytes 1540
  54.8 22.3 %copy-start.26 = (f32[128,32]{0,1:T(8,128)}, f32[128,32]{0,1:T(8,128)S(1)}, u32[]{:S(2)}) copy-start(f32[128,32]{0,1:T(8,128)S(1)} %get-tuple-element.40) | copy-start | bytes 49156
  78.7 59.7 %all-gather.12.cloned.1.call-start = ((), (), s32[]{:S(2)}) async-start(), calls=%async_computation.3 | async-start | bytes 1769472 | tf_op jit(solution)/shard_map/all_gather | solution.py:123
  79.4 121.0 %all-gather.14.cloned.1.call-start = ((), (), s32[]{:S(2)}) async-start(), calls=%async_computation.4 | async-start | bytes 3649536 | tf_op jit(solution)/shard_map/all_gather | solution.py:97
  80.0 177.5 %all-gather.16.cloned.1.call-start = ((), (), s32[]{:S(2)}) async-start(), calls=%async_computation.5 | async-start | bytes 1824768 | tf_op jit(solution)/shard_map/all_gather | solution.py:98
  80.6 223.9 %all-gather.18.cloned.1.call-start = ((), (), s32[]{:S(2)}) async-start(), calls=%async_computation.6 | async-start | bytes 1769472 | tf_op jit(solution)/shard_map/all_gather | solution.py:203
  80.7 1.3 collective-permute-start
  82.0 4.5 collective-permute-start.1
  86.5 16.8 %collective-permute-start.2 = (bf16[96,768]{1,0:T(8,128)(2,1)S(1)}, bf16[96,768]{1,0:T(8,128)(2,1)S(1)}, u32[]{:S(2)}, u32[]{:S(2)}) collective-permute-start(bf16[96,768]{1,0:T(8,128)(2,1)S(1)} %maximum_select_fusion.5), channel_id=1, source_target_pairs={{0,4},{1,5},{2,6},{3,7},{4,0},{5,1},{6,2},{7,3},{8,12},{9,13},{10,... | collective-permute-start | bytes 442376 | tf_op jit(solution)/shard_map/ppermute | solution.py:18
  103.3 8.7 %collective-permute-start.3 = (bf16[192,768]{1,0:T(8,128)(2,1)S(1)}, bf16[192,768]{1,0:T(8,128)(2,1)S(1)}, u32[]{:S(2)}, u32[]{:S(2)}) collective-permute-start(bf16[192,768]{1,0:T(8,128)(2,1)S(1)} %maximum_select_fusion.2), channel_id=1, source_target_pairs={{0,8},{1,9},{2,10},{3,11},{4,12},{5,13},{6,14},{7,15},{8,0},{9,1},... | collective-permute-start | bytes 884744 | tf_op jit(solution)/shard_map/ppermute | solution.py:18
  112.2 32.7 %collective-permute-start.4 = (bf16[384,768]{1,0:T(8,128)(2,1)S(1)}, bf16[384,768]{1,0:T(8,128)(2,1)S(1)}, u32[]{:S(2)}, u32[]{:S(2)}) collective-permute-start(bf16[384,768]{1,0:T(8,128)(2,1)S(1)} %maximum_select_fusion.1), channel_id=1, source_target_pairs={{0,16},{1,17},{2,18},{3,19},{4,20},{5,21},{6,22},{7,23},{8,24},{9,... | collective-permute-start | bytes 1769480 | tf_op jit(solution)/shard_map/ppermute | solution.py:18
  114.5 202.5 %all-gather.20.cloned.1.call-start = ((), (), s32[]{:S(2)}) async-start(), calls=%async_computation.7 | async-start | bytes 1769472 | tf_op jit(solution)/shard_map/all_gather | solution.py:204
  119.7 146.2 %copy-start.28 = (f32[12,128]{1,0:T(8,128)}, f32[12,128]{1,0:T(8,128)S(1)}, u32[]{:S(2)}) copy-start(f32[12,128]{1,0:T(8,128)S(1)} %get-tuple-element.36) | copy-start | bytes 18436
  145.5 116.0 %copy-start.1 = (f32[128,768]{1,0:T(8,128)}, f32[128,768]{1,0:T(8,128)S(1)}, u32[]{:S(2)}) copy-start(f32[128,768]{1,0:T(8,128)S(1)} %get-tuple-element.44) | copy-start | bytes 1179652
  145.5 116.0 %copy-start.31 = (f32[128]{0:T(128)}, f32[128]{0:T(128)S(1)}, u32[]{:S(2)}) copy-start(f32[128]{0:T(128)S(1)} %broadcast_multiply_fusion.5) | copy-start | bytes 1540
  145.7 115.8 %copy-start.35 = (f32[128]{0:T(128)}, f32[128]{0:T(128)S(1)}, u32[]{:S(2)}) copy-start(f32[128]{0:T(128)S(1)} %add_rsqrt_fusion) | copy-start | bytes 1540
  145.8 111.8 %copy-start.18 = (bf16[1,128,768]{2,1,0:T(8,128)(2,1)S(1)}, bf16[1,128,768]{2,1,0:T(8,128)(2,1)}, u32[]{:S(2)}) copy-start(bf16[1,128,768]{2,1,0:T(8,128)(2,1)} %param.9) | copy-start | bytes 589828
  203.1 58.4 %copy-start.7 = (f32[128,2304]{1,0:T(8,128)}, f32[128,2304]{1,0:T(8,128)S(1)}, u32[]{:S(2)}) copy-start(f32[128,2304]{1,0:T(8,128)S(1)} %fusion.83) | copy-start | bytes 3538948
  261.8 34.6 %copy-start.11 = (f32[128,768]{1,0:T(8,128)}, f32[128,768]{1,0:T(8,128)S(1)}, u32[]{:S(2)}) copy-start(f32[128,768]{1,0:T(8,128)S(1)} %multiply_add_fusion) | copy-start | bytes 1179652
  263.1 317.6 %reduce-scatter.2.cloned.1.call-start = ((), (), s32[]{:S(2)}) async-start(), calls=%async_computation.8 | async-start | bytes 21086208 | tf_op jit(solution)/shard_map/reduce_scatter | solution.py:248
  265.0 31.4 %copy-start.19 = (bf16[128,768]{0,1:T(8,128)(2,1)}, bf16[128,768]{0,1:T(8,128)(2,1)S(1)}, u32[]{:S(2)}) copy-start(bf16[128,768]{0,1:T(8,128)(2,1)S(1)} %copy.28) | copy-start | bytes 589828
  (27 other events, 82.0 us)
Sparse Core Ops, SparseCore 0:
  11.0 62.9 all-gather.7
  78.8 31.5 all-gather.9
  112.6 25.7 all-gather.11
  141.2 59.1 all-gather.13
  203.1 54.3 all-gather.15
  259.6 26.2 all-gather.17
  288.1 24.1 all-gather.19
  365.6 215.0 reduce-scatter.1
